TPU v7x, 32 devices: a whole 2x2x4 slice. The times are simulated.
32 devices in a mesh: row: 4 (over y, x), col: 8 (over z, core).
Axes of the slice: x: 2, y: 2, z: 4, core: 2. Of those that a mesh axis runs over, the one named last changes fastest.
Arguments:
- trail: float32 [2, 4, 512, 2, 8, 512], P(None, 'row', None, None, 'col'), may hold values from -6 to 6
- panel: float32 [2, 4, 512, 512], P(None, 'row', None, 'col'), may hold values from -6 to 6
- row_basis: float32 [2, 4, 64, 512], P(None, 'row', None, 'col'), may hold values from -0.75 to 0.75
- row_coeff: float32 [2, 4, 64, 512], P(None, 'row', None, 'col'), may hold values from -0.25 to 0.25
- col_basis: float32 [2, 8, 64, 512], P(None, 'col', None, 'row'), may hold values from -0.75 to 0.75
- col_scaled: float32 [2, 8, 64, 512], P(None, 'col', None, 'row'), may hold values from -0.25 to 0.25
- pivot_basis: float32 [64, 512], P(None, 'col'), may hold values from -0.75 to 0.75
- pivot_scaled: float32 [64, 512], replicated, may hold values from -0.25 to 0.25
- sketch: float32 [64, 512], replicated, may hold values from -6 to 6
- perm: int32 [512], replicated, may hold values from 0 to 511, each once
- pair_kind: int32 [256], replicated, may hold values from 0 to 1
- pivot_values: float32 [3, 256], replicated, may hold values from -3 to 3, as said below
Outputs:
- trail_out: float32 [2, 4, 512, 2, 8, 512], P(None, 'row', None, None, 'col')
- basis_out: float32 [2, 4, 64, 512], P(None, 'row')
- coeff_out: float32 [2, 4, 64, 512], P(None, 'row')
Inputs may be any that keep to these rules, and one draw needn't show every extreme that they name: `pivot_values`: rows 0 and 1 have magnitudes between 0.5 and 0.7; row 2 has magnitude 1.2 or more.
All inputs are finite; a program needn't handle non-finite values.
Results may differ from a plain program's by a relative error of at most 0.00013.
Values sent between devices are 32-bit elements; how exact they have to be, the bound alone decides.
No kernel may reach another device: no remote copies, remote signals or barrier semaphores. Data moves between devices by JAX's collectives and lax.ppermute only.
A program may use at most 64 MiB of HBM per device.

v0:
```python
import jax
import jax.numpy as jnp
from jax import lax
from jax.sharding import PartitionSpec as P


def pair_apply(rows, pair_kind, pivot_values):
    shaped = rows.reshape(rows.shape[:-1] + (rows.shape[-1] // 2, 2))
    first_in = shaped[..., 0]
    second_in = shaped[..., 1]
    diag_one = pivot_values[0]
    diag_two = pivot_values[1]
    offdiag = pivot_values[2]
    determinant = diag_one * diag_two - offdiag * offdiag
    twin = pair_kind == 1
    first = jnp.where(
        twin, (first_in * diag_two - second_in * offdiag) / determinant, first_in / diag_one
    )
    second = jnp.where(
        twin, (second_in * diag_one - first_in * offdiag) / determinant, second_in / diag_two
    )
    return jnp.stack([first, second], axis=-1).reshape(rows.shape)


def tri_solve(lower, rhs):
    return jax.vmap(lambda low, right: jax.scipy.linalg.solve_triangular(low, right, lower=True))(
        lower, rhs
    )


def body(
    trail,
    panel,
    row_basis,
    row_coeff,
    col_basis,
    col_scaled,
    pivot_basis,
    pivot_scaled,
    sketch,
    perm,
    pair_kind,
    pivot_values,
):
    highest = lax.Precision.HIGHEST
    width = sketch.shape[1]
    block = panel.shape[3]
    xrows, yrows = (
        lax.all_gather(row_basis, "col", axis=3, tiled=True),
        lax.all_gather(row_coeff, "col", axis=3, tiled=True),
    )
    zcols, gcols = (
        lax.all_gather(col_basis, "row", axis=3, tiled=True),
        lax.all_gather(col_scaled, "row", axis=3, tiled=True),
    )
    xrows = xrows[:, 0]
    yrows = yrows[:, 0]
    zcols = zcols[:, 0]
    gcols = gcols[:, 0]
    core = jnp.einsum("arp,bsp->arbs", yrows, gcols, precision=highest)
    left = jnp.einsum("arp,arbs->apbs", xrows, core, precision=highest)
    change = jnp.einsum("apbs,bsq->apbq", left, zcols, precision=highest)
    trail_out = trail - change[:, None, :, :, None, :]
    pcore = jnp.einsum("arp,sp->ars", yrows, pivot_scaled, precision=highest)
    pleft = jnp.einsum("arp,ars->aps", xrows, pcore, precision=highest)
    updated = panel[:, 0] - jnp.einsum("aps,sq->apq", pleft, pivot_basis, precision=highest)
    scaled_t = pair_apply(sketch, pair_kind, pivot_values)
    column_ids = lax.axis_index("col") * block + jnp.arange(block, dtype=jnp.int32)
    selector = (perm[:, None] == column_ids[None, :]).astype(jnp.float32)
    local_sketch = jnp.dot(scaled_t, selector, precision=highest)
    partial_range = jnp.einsum("apq,rq->arp", updated, local_sketch, precision=highest)
    range_t = lax.psum(partial_range, "col")
    gram = jnp.einsum("arp,asp->ars", range_t, range_t, precision=highest) / width
    basis = tri_solve(jnp.linalg.cholesky(gram), range_t)
    projected_part = jnp.einsum("arp,apq->arq", basis, updated, precision=highest)
    projected = lax.all_gather(projected_part, "col", axis=2, tiled=True)
    permuted = jnp.take(projected, perm, axis=2)
    coeff = pair_apply(permuted, pair_kind, pivot_values) / jnp.sqrt(jnp.float32(width))
    return (trail_out, basis[:, None], coeff[:, None])


def solution(mesh):
    return jax.shard_map(
        body,
        mesh=mesh,
        in_specs=(
            P(None, "row", None, None, "col", None),
            P(None, "row", None, "col"),
            P(None, "row", None, "col"),
            P(None, "row", None, "col"),
            P(None, "col", None, "row"),
            P(None, "col", None, "row"),
            P(None, "col"),
            P(),
            P(),
            P(),
            P(),
            P(),
        ),
        out_specs=(
            P(None, "row", None, None, "col", None),
            P(None, "row", None, None),
            P(None, "row", None, None),
        ),
        check_vma=False,
    )
```

profile of v0, /device:TPU:0, one launch (start us, length us, event | category | flops | bytes accessed | tf_op | source)
XLA Modules:
  0.0 159.1 jit_solution(12313392400558865005)
XLA Ops:
  7.2 0.0 copy-start
  7.2 0.0 copy-start.6
  7.2 0.0 copy-start.5
  7.2 0.0 copy-start.2
  7.2 0.0 copy-start.3
  7.2 0.0 copy-start.4
  7.2 0.0 all-reduce.2.cloned.1.call-start
  7.3 0.8 broadcast_compare_fusion
  8.1 0.8 fusion.16
  8.9 0.9 copy.54
  9.8 0.9 copy.51
  10.8 1.0 copy.59
  11.8 16.5 %all_gather.15 = f32[2,1,64,512]{2,0,1,3:T(2,128)S(1)} all-gather(f32[2,1,64,64]{2,0,1,3:T(2,128)S(1)} %copy.51), channel_id=1, replica_groups=mesh['row'=4,'col'=8] {'col'}, dimensions={3}, use_global_device_ids=true | all-gather | bytes 294912 | tf_op jit(solution)/shard_map/all_gather | solution.py:50
  28.3 0.2 copy.52
  28.5 14.8 %all_gather.17 = f32[2,1,64,512]{2,0,1,3:T(2,128)S(1)} all-gather(f32[2,1,64,64]{2,0,1,3:T(2,128)S(1)} %copy.54), channel_id=1, replica_groups=mesh['row'=4,'col'=8] {'col'}, dimensions={3}, use_global_device_ids=true | all-gather | bytes 294912 | tf_op jit(solution)/shard_map/all_gather | solution.py:49
  43.3 0.2 copy.55
  43.5 2.2 %broadcast_select_fusion.4 = (f32[64,256,1]{0,2,1:T(1,128)S(1)}, f32[64,256,1]{0,2,1:T(1,128)S(1)}) fusion(pred[256]{0:T(512)(128)(4,1)S(1)} %broadcast_compare_fusion, f32[64,256,2]{0,2,1:T(2,128)S(1)} %bitcast.82, f32[256]{0:T(256)S(1)} %bitcast.90, f32[256]{0:T(256)S(1)} %bitcast.96, f32[256]{0:T(256)S(1)} %bitcast.93, f32[256]{0:T(256)S(1)} %bitcast.87), kind=kLoop, calls=%fused_computation.21 | loop fusion | flops 196608 | bytes 266496 | tf_op jit(solution)/shard_map/jit(_where)/select_n | solution.py:16
  45.7 0.3 pad_maximum_fusion
  46.0 0.0 copy-done
  46.0 0.5 fusion.6
  46.5 0.4 convolution_bitcast_fusion.2
  46.8 0.0 copy-done.6
  46.8 0.5 convolution_bitcast_fusion.3
  47.3 0.0 copy-done.5
  47.3 0.0 copy-done.2
  47.3 0.4 convolution_subtract_fusion
  47.7 1.1 convolution_bitcast_fusion.1
  48.8 0.0 all-reduce.2.cloned.1.call-update
  48.9 0.0 copy-done.3
  48.9 10.3 %all_gather.18 = f32[2,1,64,512]{3,2,0,1:T(8,128)S(1)} all-gather(f32[2,1,64,128]{3,2,0,1:T(8,128)S(1)} %bitcast.85), channel_id=1, replica_groups=mesh['row'=4,'col'=8] {'row'}, dimensions={3}, use_global_device_ids=true | all-gather | bytes 327680 | tf_op jit(solution)/shard_map/all_gather | solution.py:53
  59.2 0.0 copy-done.4
  59.2 10.2 %all_gather.16 = f32[2,1,64,512]{3,2,0,1:T(8,128)S(1)} all-gather(f32[2,1,64,128]{3,2,0,1:T(8,128)S(1)} %bitcast.86), channel_id=1, replica_groups=mesh['row'=4,'col'=8] {'row'}, dimensions={3}, use_global_device_ids=true | all-gather | bytes 327680 | tf_op jit(solution)/shard_map/all_gather | solution.py:54
  69.4 0.5 fusion.1
  69.9 0.6 convolution_bitcast_fusion
  70.5 7.2 %bitcast_subtract_fusion = f32[2,1,512,2,1,512]{5,2,0,3,4,1:T(8,128)} fusion(f32[2,1,512,2,1,512]{5,4,3,2,1,0:T(1,128)} %param.12, f32[2,512,2,64]{1,3,0,2:T(8,128)S(1)} %convolution_bitcast_fusion, f32[2,1,64,512]{3,2,0,1:T(8,128)S(1)} %all_gather.18), kind=kOutput, calls=%fused_computation.1 | convolution fusion | flops 806354944 | bytes 9175040 | tf_op jit(solution)/shard_map/apbs,bsq->apbq/dot_general | solution.py:62
  77.7 0.2 broadcast_in_dim.45
  77.9 8.5 %copy.66 = f32[2,1,512,2,1,512]{5,4,3,2,1,0:T(1,128)} copy(f32[2,1,512,2,1,512]{5,2,0,3,4,1:T(8,128)} %bitcast_subtract_fusion) | data formatting | bytes 8388608
  86.4 19.4 %all-reduce.2.cloned.1.call-done = f32[2,64,512]{2,1,0:T(8,128)} async-done(((f32[2,64,512]{2,1,0:T(8,128)}), f32[2,64,512]{2,1,0:T(8,128)}) %all-reduce.2.cloned.1.call-update) | async-done | bytes 262160 | tf_op jit(solution)/shard_map/psum | solution.py:72
  105.8 1.4 fusion.17
  107.2 0.1 copy.62
  107.3 11.7 %custom-call.8 = f32[2,64,64]{2,1,0:T(8,128)S(1)} custom-call(f32[2,64,64]{2,1,0:T(8,128)S(1)} %fusion.14), custom_call_target="Cholesky" | custom-call | tf_op jit(solution)/shard_map/jit(cholesky)/cholesky | solution.py:74
  119.1 0.1 compare_reduce_fusion
  119.2 0.1 select_bitcast_fusion
  119.3 9.8 %custom-call.9 = f32[2,1,64,64]{2,3,1,0:T(8,128)S(1)} custom-call(f32[2,1,64,64]{3,2,1,0:T(8,128)S(1)} %select_bitcast_fusion), custom_call_target="InvertDiagBlocksLowerTriangular" | custom-call | tf_op jit(solution)/shard_map/vmap(jit(_solve_triangular))/triangular_solve | solution.py:26
  129.1 1.4 fusion.12
  130.5 0.0 copy-start.1
  130.5 0.4 fusion.18
  130.9 0.1 copy.64
  131.0 15.1 %all_gather.19 = f32[2,64,512]{1,0,2:T(2,128)S(1)} all-gather(f32[2,64,64]{1,0,2:T(2,128)S(1)} %copy.64), channel_id=1, replica_groups=mesh['row'=4,'col'=8] {'col'}, dimensions={2}, use_global_device_ids=true | all-gather | bytes 294912 | tf_op jit(solution)/shard_map/all_gather | solution.py:76
  146.1 2.1 %gather_fusion = f32[512,2,64]{2,1,0:T(2,128)S(1)} fusion(f32[2,64,512]{1,0,2:T(2,128)S(1)} %all_gather.19, s32[1024]{0:T(1024)S(1)} %pad_clamp_fusion), kind=kCustom, calls=%fused_computation | custom fusion | bytes 526336 | tf_op jit(solution)/shard_map/jit(_take)/gather | solution.py:77
  148.2 0.4 broadcast_select_fusion.2
  148.6 2.2 %broadcast_select_fusion.1 = (f32[2,64,256,1]{1,3,2,0:T(1,128)S(1)}, f32[2,64,256,1]{1,3,2,0:T(1,128)S(1)}) fusion(pred[256]{0:T(512)(128)(4,1)S(1)} %broadcast_compare_fusion, f32[2,64,256,2]{1,3,2,0:T(2,128)S(1)} %broadcast_select_fusion.2, f32[256]{0:T(256)S(1)} %bitcast.92, f32[256]{0:T(256)S(1)} %multiply_subtract_fusion, f32[256]{0:T(256)S(1)} %bitcast.95, ...), kind=kLoop, calls=%fused_computation.9 | loop fusion | flops 393216 | bytes 528640 | tf_op jit(solution)/shard_map/jit(_where)/select_n | solution.py:16
  150.8 0.6 maximum_multiply_fusion
  151.4 0.9 copy.68
  152.3 0.0 copy-done.1
  (10 shorter events, 0.1 us)
Async XLA Ops:
  7.2 38.8 %copy-start = (f32[64,512]{1,0:T(8,128)S(1)}, f32[64,512]{1,0:T(8,128)}, u32[]{:S(2)}) copy-start(f32[64,512]{1,0:T(8,128)} %param.19) | copy-start | bytes 393220
  7.2 39.7 %copy-start.6 = (s32[512]{0:T(512)S(1)}, s32[512]{0:T(512)}, u32[]{:S(2)}) copy-start(s32[512]{0:T(512)} %param.21) | copy-start | bytes 6148
  7.2 40.1 %copy-start.5 = (f32[64,64]{1,0:T(8,128)S(1)}, f32[64,64]{1,0:T(8,128)}, u32[]{:S(2)}) copy-start(f32[64,64]{1,0:T(8,128)} %param.18) | copy-start | bytes 49156
  7.2 40.1 %copy-start.2 = (f32[2,1,512,64]{2,3,1,0:T(8,128)S(1)}, f32[2,1,512,64]{2,3,1,0:T(8,128)}, u32[]{:S(2)}) copy-start(f32[2,1,512,64]{2,3,1,0:T(8,128)} %param.13) | copy-start | bytes 786436
  7.2 41.7 %copy-start.3 = (f32[2,1,64,128]{3,2,1,0:T(8,128)S(1)}, f32[2,1,64,128]{3,2,1,0:T(8,128)}, u32[]{:S(2)}) copy-start(f32[2,1,64,128]{3,2,1,0:T(8,128)} %param.16) | copy-start | bytes 196612
  7.2 52.0 %copy-start.4 = (f32[2,1,64,128]{3,2,1,0:T(8,128)S(1)}, f32[2,1,64,128]{3,2,1,0:T(8,128)}, u32[]{:S(2)}) copy-start(f32[2,1,64,128]{3,2,1,0:T(8,128)} %param.17) | copy-start | bytes 196612
  7.2 98.6 %all-reduce.2.cloned.1.call-start = ((), (), s32[]{:S(2)}) async-start(), calls=%async_computation | async-start | bytes 524288 | tf_op jit(solution)/shard_map/psum | solution.py:72
  130.5 21.8 %copy-start.1 = (f32[2,64,512]{2,1,0:T(8,128)}, f32[2,64,512]{2,1,0:T(8,128)S(1)}, u32[]{:S(2)}) copy-start(f32[2,64,512]{2,1,0:T(8,128)S(1)} %fusion.12) | copy-start | bytes 786436
Sparse Core Ops, SparseCore 0:
  49.0 56.7 all-reduce.1
where the time goes:
time: 160 us; the launch traced here: 159 us
  blocking collectives  66.8 us (42%)
  other arithmetic  29.1 us (18%)
  waiting for transfers between devices  19.4 us (12%)
  local copies, waits for them, and re-layouts  15.2 us (10%)
  between operations  14.4 us (9%)
  matrix products  14.3 us (9%)
    psum x1, waiting for transfers between devices, body(): range_t = lax.psum(partial_range, 'col')  19.4 us
    all_gather x1, blocking collectives, body(): lax.all_gather(row_coeff, 'col', axis=3, tiled=True)  16.5 us
    all_gather x1, blocking collectives, body(): projected = lax.all_gather(projected_part, 'col', axis=2, tiled=True)  15.1 us
    all_gather x1, blocking collectives, body(): lax.all_gather(row_basis, 'col', axis=3, tiled=True)  14.8 us
    unnamed x19, local copies, waits for them, and re-layouts  12.3 us
    another operation x4, other arithmetic, body(): basis = tri_solve(jnp.linalg.cholesky(gram), range_t)  11.9 us
    all_gather x1, blocking collectives, body(): lax.all_gather(col_basis, 'row', axis=3, tiled=True)  10.3 us
    all_gather x1, blocking collectives, body(): lax.all_gather(col_scaled, 'row', axis=3, tiled=True)  10.2 us
  transfers between devices with their start and end apart: 1, of which 1 were waited for; matrix products, arithmetic and copies ran while one was open for 11% of the time, Pallas kernels for 0%

commit v1 on v0

--- a/solution.py
+++ b/solution.py
@@ -1,7 +1,26 @@
+import functools
 import jax
 import jax.numpy as jnp
 from jax import lax
 from jax.sharding import PartitionSpec as P
+
+
+def replace_shards_by_axis(array_in, axis_name):
+    extent = lax.axis_size(axis_name)
+    shelf = [array_in]
+    t = 0
+    while t < extent - 1:
+        block_next = lax.ppermute(
+            shelf[-1], axis_name, [(kk, (kk + 1) % extent) for kk in range(extent)]
+        )
+        shelf.append(block_next)
+        t += 1
+    y_new = jnp.concatenate(shelf[::-1], 2)
+    v1 = jnp.roll(y_new, (lax.axis_index(axis_name) + 1) * array_in.shape[2], 2)
+    return v1
+
+
+pair_page = functools.partial(replace_shards_by_axis, axis_name="col")
 
 
 def pair_apply(rows, pair_kind, pivot_values):
@@ -73,7 +92,7 @@
     gram = jnp.einsum("arp,asp->ars", range_t, range_t, precision=highest) / width
     basis = tri_solve(jnp.linalg.cholesky(gram), range_t)
     projected_part = jnp.einsum("arp,apq->arq", basis, updated, precision=highest)
-    projected = lax.all_gather(projected_part, "col", axis=2, tiled=True)
+    projected = pair_page(projected_part)
     permuted = jnp.take(projected, perm, axis=2)
     coeff = pair_apply(permuted, pair_kind, pivot_values) / jnp.sqrt(jnp.float32(width))
     return (trail_out, basis[:, None], coeff[:, None])

time: 160 us -> 193 us (1.21)
  waiting for transfers between devices: 19.4 us -> 67.3 us
  blocking collectives: 66.8 us -> 51.6 us
    psum x1, waiting for transfers between devices: 19.4 us -> 46 us  [body(): range_t = lax.psum(partial_range, 'col')]
    ppermute x0 -> x7, waiting for transfers between devices: none -> 21.3 us  [replace_shards_by_axis(): lax.ppermute(shelf[-1], axis_name, [(kk, (kk + 1) % extent) for kk in ran...]
    all_gather x1 -> x0, blocking collectives: 15.1 us -> none  [body(): projected = lax.all_gather(projected_part, 'col', axis=2, tiled=True)]
  transfers between devices with their start and end apart: 1 -> 8, of which waited for: 1 -> 5; matrix products, arithmetic and copies ran while one was open for 11% -> 9% of each run, Pallas kernels for 0% -> 0%
where the time goes in v1:
time: 193 us
  waiting for transfers between devices  67.3 us (35%)
  blocking collectives  51.6 us (27%)
  other arithmetic  29.1 us (15%)
  local copies, waits for them, and re-layouts  15.7 us (8%)
  between operations  14.4 us (7%)
  matrix products  14.3 us (7%)
    psum x1, waiting for transfers between devices, body(): range_t = lax.psum(partial_range, 'col')  46 us
    ppermute x7, waiting for transfers between devices, replace_shards_by_axis(): lax.ppermute(shelf[-1], axis_name, [(kk, (kk + 1) % extent) for kk in ran...  21.3 us
    all_gather x1, blocking collectives, body(): lax.all_gather(row_coeff, 'col', axis=3, tiled=True)  16.5 us
    all_gather x1, blocking collectives, body(): lax.all_gather(row_basis, 'col', axis=3, tiled=True)  14.8 us
    unnamed x19, local copies, waits for them, and re-layouts  12.3 us
    another operation x4, other arithmetic, body(): basis = tri_solve(jnp.linalg.cholesky(gram), range_t)  11.9 us
    all_gather x1, blocking collectives, body(): lax.all_gather(col_scaled, 'row', axis=3, tiled=True)  10.3 us
    all_gather x1, blocking collectives, body(): lax.all_gather(col_basis, 'row', axis=3, tiled=True)  9.99 us
  transfers between devices with their start and end apart: 8, of which 5 were waited for; matrix products, arithmetic and copies ran while one was open for 9% of the time, Pallas kernels for 0%

profile of v1, /device:TPU:0, one launch (start us, length us, event | category | flops | bytes accessed | tf_op | source)
XLA Modules:
  0.0 192.6 jit_solution(4957277382161737081)
XLA Ops:
  7.2 0.0 copy-start
  7.2 0.0 copy-start.6
  7.2 0.0 all-reduce.2.cloned.1.call-start
  7.3 0.8 broadcast_compare_fusion
  8.1 0.8 fusion.16
  8.9 0.9 copy.54
  9.8 0.9 copy.51
  10.7 1.0 copy.59
  11.8 16.5 %all_gather.12 = f32[2,1,64,512]{2,0,1,3:T(2,128)S(1)} all-gather(f32[2,1,64,64]{2,0,1,3:T(2,128)S(1)} %copy.51), channel_id=1, replica_groups=mesh['row'=4,'col'=8] {'col'}, dimensions={3}, use_global_device_ids=true | all-gather | bytes 294912 | tf_op jit(solution)/shard_map/all_gather | solution.py:69
  28.3 0.2 copy.52
  28.5 14.8 %all_gather.14 = f32[2,1,64,512]{2,0,1,3:T(2,128)S(1)} all-gather(f32[2,1,64,64]{2,0,1,3:T(2,128)S(1)} %copy.54), channel_id=1, replica_groups=mesh['row'=4,'col'=8] {'col'}, dimensions={3}, use_global_device_ids=true | all-gather | bytes 294912 | tf_op jit(solution)/shard_map/all_gather | solution.py:68
  43.3 0.2 copy.55
  43.4 0.0 copy-start.4
  43.5 2.2 %broadcast_select_fusion.4 = (f32[64,256,1]{0,2,1:T(1,128)S(1)}, f32[64,256,1]{0,2,1:T(1,128)S(1)}) fusion(pred[256]{0:T(512)(128)(4,1)S(1)} %broadcast_compare_fusion, f32[64,256,2]{0,2,1:T(2,128)S(1)} %bitcast.82, f32[256]{0:T(256)S(1)} %bitcast.90, f32[256]{0:T(256)S(1)} %bitcast.96, f32[256]{0:T(256)S(1)} %bitcast.93, f32[256]{0:T(256)S(1)} %bitcast.87), kind=kLoop, calls=%fused_computation.21 | loop fusion | flops 196608 | bytes 266496 | tf_op jit(solution)/shard_map/jit(_where)/select_n | solution.py:35
  45.6 0.3 pad_maximum_fusion
  45.9 0.5 fusion.6
  46.5 0.4 convolution_bitcast_fusion.2
  46.8 0.5 convolution_bitcast_fusion.3
  47.3 0.0 copy-done.5
  47.3 0.0 copy-done.2
  47.3 0.4 convolution_subtract_fusion
  47.7 1.1 convolution_bitcast_fusion.1
  48.8 0.0 all-reduce.2.cloned.1.call-update
  48.8 0.0 copy-done.3
  48.8 10.3 %all_gather.13 = f32[2,1,64,512]{3,2,0,1:T(8,128)S(1)} all-gather(f32[2,1,64,128]{3,2,0,1:T(8,128)S(1)} %bitcast.85), channel_id=1, replica_groups=mesh['row'=4,'col'=8] {'row'}, dimensions={3}, use_global_device_ids=true | all-gather | bytes 327680 | tf_op jit(solution)/shard_map/all_gather | solution.py:73
  59.2 0.5 fusion.1
  59.7 46.0 %all-reduce.2.cloned.1.call-done = f32[2,64,512]{2,1,0:T(8,128)} async-done(((f32[2,64,512]{2,1,0:T(8,128)}), f32[2,64,512]{2,1,0:T(8,128)}) %all-reduce.2.cloned.1.call-update) | async-done | bytes 262160 | tf_op jit(solution)/shard_map/psum | solution.py:91
  105.8 1.4 fusion.17
  107.2 0.1 copy.62
  107.3 11.7 %custom-call.8 = f32[2,64,64]{2,1,0:T(8,128)S(1)} custom-call(f32[2,64,64]{2,1,0:T(8,128)S(1)} %fusion.14), custom_call_target="Cholesky" | custom-call | tf_op jit(solution)/shard_map/jit(cholesky)/cholesky | solution.py:93
  119.0 0.1 compare_reduce_fusion
  119.2 0.1 select_bitcast_fusion
  119.2 9.8 %custom-call.9 = f32[2,1,64,64]{2,3,1,0:T(8,128)S(1)} custom-call(f32[2,1,64,64]{3,2,1,0:T(8,128)S(1)} %select_bitcast_fusion), custom_call_target="InvertDiagBlocksLowerTriangular" | custom-call | tf_op jit(solution)/shard_map/vmap(jit(_solve_triangular))/triangular_solve | solution.py:45
  129.1 1.4 fusion.12
  130.5 0.0 copy-start.1
  130.5 0.4 fusion.18
  130.9 0.1 collective-permute-start
  130.9 0.6 convolution_bitcast_fusion
  131.5 4.9 %collective-permute-done = f32[2,64,64]{2,1,0:T(8,128)S(1)} collective-permute-done((f32[2,64,64]{2,1,0:T(8,128)S(1)}, f32[2,64,64]{2,1,0:T(8,128)S(1)}, u32[]{:S(2)}, u32[]{:S(2)}) %collective-permute-start) | collective-permute-done | bytes 32800 | tf_op jit(solution)/shard_map/ppermute | solution.py:13
  136.4 0.0 collective-permute-start.1
  136.4 10.0 %all_gather.15 = f32[2,1,64,512]{3,2,0,1:T(8,128)S(1)} all-gather(f32[2,1,64,128]{3,2,0,1:T(8,128)S(1)} %bitcast.86), channel_id=1, replica_groups=mesh['row'=4,'col'=8] {'row'}, dimensions={3}, use_global_device_ids=true | all-gather | bytes 327680 | tf_op jit(solution)/shard_map/all_gather | solution.py:72
  146.4 0.0 collective-permute-done.1
  146.4 0.0 collective-permute-start.2
  146.4 7.2 %bitcast_subtract_fusion = f32[2,1,512,2,1,512]{5,2,0,3,4,1:T(8,128)} fusion(f32[2,1,512,2,1,512]{5,4,3,2,1,0:T(1,128)} %param.12, f32[2,512,2,64]{1,3,0,2:T(8,128)S(1)} %convolution_bitcast_fusion, f32[2,1,64,512]{3,2,0,1:T(8,128)S(1)} %all_gather.15), kind=kOutput, calls=%fused_computation.1 | convolution fusion | flops 806354944 | bytes 9175040 | tf_op jit(solution)/shard_map/apbs,bsq->apbq/dot_general | solution.py:81
  153.6 0.0 copy-done.1
  153.6 0.0 collective-permute-done.2
  153.6 0.1 collective-permute-start.3
  153.7 5.4 %collective-permute-done.3 = f32[2,64,64]{2,1,0:T(8,128)S(1)} collective-permute-done((f32[2,64,64]{2,1,0:T(8,128)S(1)}, f32[2,64,64]{2,1,0:T(8,128)S(1)}, u32[]{:S(2)}, u32[]{:S(2)}) %collective-permute-start.3) | collective-permute-done | bytes 32800 | tf_op jit(solution)/shard_map/ppermute | solution.py:13
  159.1 0.0 collective-permute-start.4
  159.1 5.5 %collective-permute-done.4 = f32[2,64,64]{2,1,0:T(8,128)S(1)} collective-permute-done((f32[2,64,64]{2,1,0:T(8,128)S(1)}, f32[2,64,64]{2,1,0:T(8,128)S(1)}, u32[]{:S(2)}, u32[]{:S(2)}) %collective-permute-start.4) | collective-permute-done | bytes 32800 | tf_op jit(solution)/shard_map/ppermute | solution.py:13
  164.6 0.0 collective-permute-start.5
  164.6 5.5 %collective-permute-done.5 = f32[2,64,64]{2,1,0:T(8,128)S(1)} collective-permute-done((f32[2,64,64]{2,1,0:T(8,128)S(1)}, f32[2,64,64]{2,1,0:T(8,128)S(1)}, u32[]{:S(2)}, u32[]{:S(2)}) %collective-permute-start.5) | collective-permute-done | bytes 32800 | tf_op jit(solution)/shard_map/ppermute | solution.py:13
  170.1 0.0 collective-permute-start.6
  170.1 0.2 broadcast_in_dim.45
  170.3 8.5 %copy.66 = f32[2,1,512,2,1,512]{5,4,3,2,1,0:T(1,128)} copy(f32[2,1,512,2,1,512]{5,2,0,3,4,1:T(8,128)} %bitcast_subtract_fusion) | data formatting | bytes 8388608
  178.8 0.0 collective-permute-done.6
  178.8 0.3 concatenate.6
  179.1 0.1 constant_dynamic-slice_fusion
  179.2 0.2 copy.64
  179.5 2.1 %gather_fusion = f32[512,2,64]{2,1,0:T(2,128)S(1)} fusion(f32[2,64,512]{1,0,2:T(2,128)S(1)} %copy.64, s32[1024]{0:T(1024)S(1)} %pad_clamp_fusion), kind=kCustom, calls=%fused_computation | custom fusion | bytes 526336 | tf_op jit(solution)/shard_map/jit(_take)/gather | solution.py:96
  181.6 0.4 broadcast_select_fusion.2
  182.0 2.2 %broadcast_select_fusion.1 = (f32[2,64,256,1]{1,3,2,0:T(1,128)S(1)}, f32[2,64,256,1]{1,3,2,0:T(1,128)S(1)}) fusion(pred[256]{0:T(512)(128)(4,1)S(1)} %broadcast_compare_fusion, f32[2,64,256,2]{1,3,2,0:T(2,128)S(1)} %broadcast_select_fusion.2, f32[256]{0:T(256)S(1)} %bitcast.92, f32[256]{0:T(256)S(1)} %multiply_subtract_fusion, f32[256]{0:T(256)S(1)} %bitcast.95, ...), kind=kLoop, calls=%fused_computation.9 | loop fusion | flops 393216 | bytes 528640 | tf_op jit(solution)/shard_map/jit(_where)/select_n | solution.py:35
  184.2 0.6 maximum_multiply_fusion
  184.8 0.9 copy.68
  (16 shorter events, 0.1 us)
Async XLA Ops:
  7.2 38.8 %copy-start = (f32[64,512]{1,0:T(8,128)S(1)}, f32[64,512]{1,0:T(8,128)}, u32[]{:S(2)}) copy-start(f32[64,512]{1,0:T(8,128)} %param.19) | copy-start | bytes 393220
  7.2 39.6 %copy-start.6 = (s32[512]{0:T(512)S(1)}, s32[512]{0:T(512)}, u32[]{:S(2)}) copy-start(s32[512]{0:T(512)} %param.21) | copy-start | bytes 6148
  7.2 40.1 %copy-start.5 = (f32[64,64]{1,0:T(8,128)S(1)}, f32[64,64]{1,0:T(8,128)}, u32[]{:S(2)}) copy-start(f32[64,64]{1,0:T(8,128)} %param.18) | copy-start | bytes 49156
  7.2 40.1 %copy-start.2 = (f32[2,1,512,64]{2,3,1,0:T(8,128)S(1)}, f32[2,1,512,64]{2,3,1,0:T(8,128)}, u32[]{:S(2)}) copy-start(f32[2,1,512,64]{2,3,1,0:T(8,128)} %param.13) | copy-start | bytes 786436
  7.2 41.6 %copy-start.3 = (f32[2,1,64,128]{3,2,1,0:T(8,128)S(1)}, f32[2,1,64,128]{3,2,1,0:T(8,128)}, u32[]{:S(2)}) copy-start(f32[2,1,64,128]{3,2,1,0:T(8,128)} %param.17) | copy-start | bytes 196612
  7.2 98.5 %all-reduce.2.cloned.1.call-start = ((), (), s32[]{:S(2)}) async-start(), calls=%async_computation | async-start | bytes 524288 | tf_op jit(solution)/shard_map/psum | solution.py:91
  43.4 93.0 %copy-start.4 = (f32[2,1,64,128]{3,2,1,0:T(8,128)S(1)}, f32[2,1,64,128]{3,2,1,0:T(8,128)}, u32[]{:S(2)}) copy-start(f32[2,1,64,128]{3,2,1,0:T(8,128)} %param.16) | copy-start | bytes 196612
  130.5 23.1 %copy-start.1 = (f32[2,64,512]{2,1,0:T(8,128)}, f32[2,64,512]{2,1,0:T(8,128)S(1)}, u32[]{:S(2)}) copy-start(f32[2,64,512]{2,1,0:T(8,128)S(1)} %fusion.12) | copy-start | bytes 786436
  130.9 5.5 %collective-permute-start = (f32[2,64,64]{2,1,0:T(8,128)S(1)}, f32[2,64,64]{2,1,0:T(8,128)S(1)}, u32[]{:S(2)}, u32[]{:S(2)}) collective-permute-start(f32[2,64,64]{2,1,0:T(8,128)S(1)} %fusion.18), channel_id=1, source_target_pairs={{0,1},{1,2},{2,3},{3,4},{4,5},{5,6},{6,7},{7,0},{8,9},{9,10},{10,1... | collective-permute-start | bytes 98312 | tf_op jit(solution)/shard_map/ppermute | solution.py:13
  136.4 10.0 %collective-permute-start.1 = (f32[2,64,64]{2,1,0:T(8,128)S(1)}, f32[2,64,64]{2,1,0:T(8,128)S(1)}, u32[]{:S(2)}, u32[]{:S(2)}) collective-permute-start(f32[2,64,64]{2,1,0:T(8,128)S(1)} %collective-permute-done), channel_id=1, source_target_pairs={{0,1},{1,2},{2,3},{3,4},{4,5},{5,6},{6,7},{7,0},{8,9},{9,10},{10,1... | collective-permute-start | bytes 98312 | tf_op jit(solution)/shard_map/ppermute | solution.py:13
  146.4 7.2 %collective-permute-start.2 = (f32[2,64,64]{2,1,0:T(8,128)S(1)}, f32[2,64,64]{2,1,0:T(8,128)S(1)}, u32[]{:S(2)}, u32[]{:S(2)}) collective-permute-start(f32[2,64,64]{2,1,0:T(8,128)S(1)} %collective-permute-done.1), channel_id=1, source_target_pairs={{0,1},{1,2},{2,3},{3,4},{4,5},{5,6},{6,7},{7,0},{8,9},{9,10},{10,1... | collective-permute-start | bytes 98312 | tf_op jit(solution)/shard_map/ppermute | solution.py:13
  153.6 5.5 %collective-permute-start.3 = (f32[2,64,64]{2,1,0:T(8,128)S(1)}, f32[2,64,64]{2,1,0:T(8,128)S(1)}, u32[]{:S(2)}, u32[]{:S(2)}) collective-permute-start(f32[2,64,64]{2,1,0:T(8,128)S(1)} %collective-permute-done.2), channel_id=1, source_target_pairs={{0,1},{1,2},{2,3},{3,4},{4,5},{5,6},{6,7},{7,0},{8,9},{9,10},{10,1... | collective-permute-start | bytes 98312 | tf_op jit(solution)/shard_map/ppermute | solution.py:13
  159.1 5.5 %collective-permute-start.4 = (f32[2,64,64]{2,1,0:T(8,128)S(1)}, f32[2,64,64]{2,1,0:T(8,128)S(1)}, u32[]{:S(2)}, u32[]{:S(2)}) collective-permute-start(f32[2,64,64]{2,1,0:T(8,128)S(1)} %collective-permute-done.3), channel_id=1, source_target_pairs={{0,1},{1,2},{2,3},{3,4},{4,5},{5,6},{6,7},{7,0},{8,9},{9,10},{10,1... | collective-permute-start | bytes 98312 | tf_op jit(solution)/shard_map/ppermute | solution.py:13
  164.6 5.5 %collective-permute-start.5 = (f32[2,64,64]{2,1,0:T(8,128)S(1)}, f32[2,64,64]{2,1,0:T(8,128)S(1)}, u32[]{:S(2)}, u32[]{:S(2)}) collective-permute-start(f32[2,64,64]{2,1,0:T(8,128)S(1)} %collective-permute-done.4), channel_id=1, source_target_pairs={{0,1},{1,2},{2,3},{3,4},{4,5},{5,6},{6,7},{7,0},{8,9},{9,10},{10,1... | collective-permute-start | bytes 98312 | tf_op jit(solution)/shard_map/ppermute | solution.py:13
  170.1 8.7 %collective-permute-start.6 = (f32[2,64,64]{2,1,0:T(8,128)S(1)}, f32[2,64,64]{2,1,0:T(8,128)S(1)}, u32[]{:S(2)}, u32[]{:S(2)}) collective-permute-start(f32[2,64,64]{2,1,0:T(8,128)S(1)} %collective-permute-done.5), channel_id=1, source_target_pairs={{0,1},{1,2},{2,3},{3,4},{4,5},{5,6},{6,7},{7,0},{8,9},{9,10},{10,1... | collective-permute-start | bytes 98312 | tf_op jit(solution)/shard_map/ppermute | solution.py:13
Sparse Core Ops, SparseCore 0:
  49.0 56.7 all-reduce.1
